TPU v7x, 32 devices: a whole 2x2x4 slice. The times are simulated.
32 devices in a mesh: grp: 4 (over y, x), blk: 8 (over z, core).
Axes of the slice: x: 2, y: 2, z: 4, core: 2. Of those that a mesh axis runs over, the one named last changes fastest.
Arguments:
- student: bfloat16 [6144, 1024], P(('grp', 'blk')), parts along dimension 0, may hold values from -6 to 6
- teacher: bfloat16 [6144, 1024], P(('grp', 'blk')), parts along dimension 0, may hold values from -6 to 6
Outputs:
- grad_student: float32 [6144, 1024], P(('grp', 'blk')), parts along dimension 0
There are 4 independent parts, one for each index of `grp`. A program takes and returns all parts, laid end to end along the dimension named above; each array names one. Nothing has to cross between parts.
All inputs are finite; a program needn't handle non-finite values.
Results may differ from a plain program's by a relative error of at most 0.01.
Values may be sent and summed in bfloat16 or wider, within the bound.
No kernel may reach another device: no remote copies, remote signals or barrier semaphores. Data moves between devices by JAX's collectives and lax.ppermute only.
A program may use at most 128 MiB of HBM per device.

v0:
```python
import jax
import jax.numpy as jnp
from jax import lax
from jax.sharding import PartitionSpec as P

D = 1024


def normalize(values):
    floats = values.astype(jnp.float32)
    norms = jnp.sqrt(jnp.sum(floats * floats, axis=1, keepdims=True) + 1e-06)
    return (floats / norms, norms)


def split_product(left, right):
    left_hi = left.astype(jnp.bfloat16)
    left_lo = (left - left_hi.astype(jnp.float32)).astype(jnp.bfloat16)
    return jnp.dot(left_hi, right, preferred_element_type=jnp.float32) + jnp.dot(
        left_lo, right, preferred_element_type=jnp.float32
    )


def body(student, teacher):
    row_count = student.shape[0]
    text_count = row_count * lax.axis_size("blk")
    s_float, norm_h = normalize(student)
    s_half = s_float.astype(jnp.bfloat16)
    t_float, teacher_norm = normalize(teacher)
    t_half = t_float.astype(jnp.bfloat16)
    s_wide = s_half.astype(jnp.float32)
    s_piece = lax.all_gather(s_half, "blk", axis=0, tiled=True)
    t_piece = lax.all_gather(t_half, "blk", axis=0, tiled=True)
    gram_s = lax.dot_general(
        s_half, s_piece, (((1,), (1,)), ((), ())), preferred_element_type=jnp.float32
    )
    gram_t = lax.dot_general(
        t_half, t_piece, (((1,), (1,)), ((), ())), preferred_element_type=jnp.float32
    )
    product = split_product(gram_s - gram_t, s_piece)
    g_s = product * (D / jnp.sqrt(jnp.float32(text_count)))
    along = jnp.sum(s_wide * g_s, axis=1, keepdims=True)
    return (g_s - s_wide * along) / norm_h


def solution(mesh):
    in_specs = (P(("grp", "blk"), None), P(("grp", "blk"), None))
    out_specs = P(("grp", "blk"), None)
    return jax.shard_map(body, mesh=mesh, in_specs=in_specs, out_specs=out_specs, check_vma=False)
```

profile of v0, /device:TPU:0, one launch (start us, length us, event | category | flops | bytes accessed | tf_op | source)
XLA Modules:
  0.0 102.9 jit_solution(4346751903632216425)
XLA Ops:
  6.5 0.0 all-gather.3.cloned.1.call-start
  6.5 1.2 %fusion.1 = f32[192]{0:T(256)S(1)} fusion(bf16[192,1024]{1,0:T(8,128)(2,1)} %param.2), kind=kLoop, calls=%fused_computation.10 | loop fusion | flops 589632 | bytes 393984 | tf_op jit(solution)/shard_map/reduce_sum | solution.py:11
  7.7 1.9 %fusion.2 = bf16[192,1024]{1,0:T(8,128)(2,1)} fusion(bf16[192,1024]{1,0:T(8,128)(2,1)} %param.2, f32[192]{0:T(256)S(1)} %add_sqrt_fusion.1), kind=kLoop, calls=%fused_computation.11 | loop fusion | flops 589824 | bytes 787200 | tf_op jit(solution)/shard_map/convert_element_type | solution.py:27
  9.6 0.0 all-gather.3.cloned.1.call-update
  9.6 0.0 all-gather.5.cloned.1.call-start
  9.7 1.2 %fusion.3 = f32[192]{0:T(256)S(1)} fusion(bf16[192,1024]{1,0:T(8,128)(2,1)} %param.3), kind=kLoop, calls=%fused_computation.12 | loop fusion | flops 589632 | bytes 393984 | tf_op jit(solution)/shard_map/reduce_sum | solution.py:11
  10.8 1.9 %fusion.4 = bf16[192,1024]{1,0:T(8,128)(2,1)} fusion(bf16[192,1024]{1,0:T(8,128)(2,1)} %param.3, f32[192]{0:T(256)S(1)} %add_sqrt_fusion), kind=kLoop, calls=%fused_computation.13 | loop fusion | flops 589824 | bytes 787200 | tf_op jit(solution)/shard_map/convert_element_type | solution.py:29
  12.7 0.0 copy-start.2
  12.7 0.0 all-gather.5.cloned.1.call-update
  12.8 38.0 %all-gather.3.cloned.1.call-done = bf16[1536,1024]{1,0:T(8,128)(2,1)} async-done(((bf16[192,1024]{1,0:T(8,128)(2,1)}), bf16[1536,1024]{1,0:T(8,128)(2,1)}) %all-gather.3.cloned.1.call-update) | async-done | bytes 3145744 | tf_op jit(solution)/shard_map/all_gather | solution.py:31
  50.7 4.2 %fusion.11 = f32[192,1536]{1,0:T(8,128)} fusion(bf16[192,1024]{1,0:T(8,128)(2,1)} %fusion.2, bf16[1536,1024]{1,0:T(8,128)(2,1)} %all-gather.3.cloned.1.call-done), kind=kOutput, calls=%fused_computation.22 | convolution fusion | flops 603979776 | bytes 4718592 | tf_op jit(solution)/shard_map/dot_general | solution.py:33
  55.0 0.0 copy-start
  55.0 34.5 %all-gather.5.cloned.1.call-done = bf16[1536,1024]{1,0:T(8,128)(2,1)} async-done(((bf16[192,1024]{1,0:T(8,128)(2,1)}), bf16[1536,1024]{1,0:T(8,128)(2,1)}) %all-gather.5.cloned.1.call-update) | async-done | bytes 3145744 | tf_op jit(solution)/shard_map/all_gather | solution.py:32
  89.5 0.0 copy-done.2
  89.5 3.4 %convolution_subtract_fusion = f32[192,1536]{1,0:T(8,128)S(1)} fusion(f32[192,1536]{1,0:T(8,128)} %fusion.11, bf16[192,1024]{1,0:T(8,128)(2,1)S(1)} %copy-done.2, bf16[1536,1024]{1,0:T(8,128)(2,1)} %all-gather.5.cloned.1.call-done), kind=kOutput, calls=%fused_computation | convolution fusion | flops 604274688 | bytes 5898240 | tf_op jit(solution)/shard_map/dot_general | solution.py:36
  92.9 0.0 copy-done
  92.9 0.0 copy-start.1
  93.0 0.8 fusion.9
  93.8 0.2 copy-done.1
  93.9 0.0 copy-start.3
  93.9 1.0 fusion.5
  94.9 0.0 copy-done.3
  94.9 1.1 %fusion.7 = f32[192,1024]{1,0:T(8,128)} fusion(f32[192,1024]{1,0:T(8,128)S(1)} %get-tuple-element.6, f32[192]{0:T(256)S(1)} %get-tuple-element.5, f32[192]{0:T(256)S(1)} %add_sqrt_fusion.1, bf16[192,1024]{1,0:T(8,128)(2,1)S(1)} %copy-done.3), kind=kLoop, calls=%fused_computation.16 | loop fusion | flops 1376256 | bytes 1967616 | tf_op jit(solution)/shard_map/div | solution.py:42
  (2 shorter events, 0.0 us)
Async XLA Ops:
  6.5 44.2 %all-gather.3.cloned.1.call-start = ((), (), s32[]{:S(2)}) async-start(), calls=%async_computation | async-start | bytes 3538944 | tf_op jit(solution)/shard_map/all_gather | solution.py:31
  9.6 79.9 %all-gather.5.cloned.1.call-start = ((), (), s32[]{:S(2)}) async-start(), calls=%async_computation.1 | async-start | bytes 3538944 | tf_op jit(solution)/shard_map/all_gather | solution.py:32
  12.7 76.8 %copy-start.2 = (bf16[192,1024]{1,0:T(8,128)(2,1)S(1)}, bf16[192,1024]{1,0:T(8,128)(2,1)}, u32[]{:S(2)}) copy-start(bf16[192,1024]{1,0:T(8,128)(2,1)} %fusion.4) | copy-start | bytes 1179652
  55.0 38.0 %copy-start = (bf16[1536,1024]{1,0:T(8,128)(2,1)S(1)}, bf16[1536,1024]{1,0:T(8,128)(2,1)}, u32[]{:S(2)}) copy-start(bf16[1536,1024]{1,0:T(8,128)(2,1)} %all-gather.3.cloned.1.call-done) | copy-start | bytes 9437188
  92.9 1.0 copy-start.1
  93.9 1.0 copy-start.3
Sparse Core Ops, SparseCore 0:
  9.7 40.9 all-gather.2
  52.4 37.1 all-gather.4
where the time goes:
time: 103 us
  waiting for transfers between devices  72.5 us (70%)
  between operations  13.4 us (13%)
  matrix products  9.43 us (9%)
  other arithmetic  7.21 us (7%)
    all_gather x1, waiting for transfers between devices, body(): s_piece = lax.all_gather(s_half, 'blk', axis=0, tiled=True)  38 us
    all_gather x1, waiting for transfers between devices, body(): t_piece = lax.all_gather(t_half, 'blk', axis=0, tiled=True)  34.5 us
    dot_general x1, matrix products, body(): lax.dot_general(s_half, s_piece, (((1,), (1,)), ((), ())), preferred_elem...  4.25 us
    dot_general x1, matrix products, body(): lax.dot_general(t_half, t_piece, (((1,), (1,)), ((), ())), preferred_elem...  3.4 us
    reduce_sum x2, other arithmetic, normalize(): norms = jnp.sqrt(jnp.sum(floats * floats, axis=1, keepdims=True) + 1e-06)  2.31 us
  transfers between devices with their start and end apart: 2, of which 2 were waited for; matrix products, arithmetic and copies ran while one was open for 7% of the time, Pallas kernels for 0%

commit v1 on v0

v1 whole, which is shorter than its diff:
```python
import functools

import jax
import jax.numpy as jnp
from jax import lax
from jax.experimental import pallas as pl
from jax.experimental.pallas import tpu as pltpu
from jax.sharding import PartitionSpec as P

CORES = 2
VMEM = pltpu.MemorySpace.VMEM
SMEM = pltpu.MemorySpace.SMEM
NT = (((1,), (1,)), ((), ()))


def normalized(ref):
    floats = ref[...].astype(jnp.float32)
    norms = jnp.sqrt(jnp.sum(floats * floats, axis=1, keepdims=True) + 1e-06)
    return (floats / norms).astype(jnp.bfloat16), norms


def accumulate(s_rows, t_rows, s_cols, t_cols, store):
    slab = s_cols.shape[0]
    for start in range(0, s_rows.shape[0], slab):
        rows = pl.ds(start, slab)
        gram = lax.dot_general(
            s_rows[rows, :], s_cols[...], NT, preferred_element_type=jnp.float32
        ) - lax.dot_general(
            t_rows[rows, :], t_cols[...], NT, preferred_element_type=jnp.float32
        )
        high = gram.astype(jnp.bfloat16)
        low = (gram - high.astype(jnp.float32)).astype(jnp.bfloat16)
        store(
            rows,
            jnp.dot(high, s_cols[...], preferred_element_type=jnp.float32)
            + jnp.dot(low, s_cols[...], preferred_element_type=jnp.float32),
        )


def first_kernel(s_own, t_own, s_other, t_other, s_rows, t_rows, norms, total):
    half = s_own.shape[0]
    own, other = pl.ds(0, half), pl.ds(half, half)
    s_rows[own, :], norm = normalized(s_own)
    norms[...] = jnp.broadcast_to(norm, norms.shape)
    t_rows[own, :], _ = normalized(t_own)
    s_rows[other, :], _ = normalized(s_other)
    t_rows[other, :], _ = normalized(t_other)

    def store(rows, value):
        total[rows, :] = value

    accumulate(s_rows, t_rows, s_rows.at[own, :], t_rows.at[own, :], store)


def step_kernel(
    low_ok, high_ok, place, s_rows, t_rows, total_in, s_right, t_right, s_left, t_left,
    total, s_raw, t_raw, s_cols, t_cols, sems,
):
    @pl.when(pl.program_id(0) == 0)
    def _():
        total[...] = total_in[...]

    def block(s_hbm, t_hbm):
        s_copy = pltpu.make_async_copy(s_hbm, s_raw, sems.at[0])
        t_copy = pltpu.make_async_copy(t_hbm, t_raw, sems.at[1])
        s_copy.start()
        t_copy.start()
        s_copy.wait()
        s_cols[...], _ = normalized(s_raw)
        t_copy.wait()
        t_cols[...], _ = normalized(t_raw)

        def store(rows, value):
            total[rows, :] += value

        accumulate(s_rows, t_rows, s_cols, t_cols, store)

    chip = place[0]

    @pl.when(chip >= low_ok)
    def _():
        block(s_right, t_right)

    @pl.when(chip <= high_ok)
    def _():
        block(s_left, t_left)


def last_kernel(scale, total, received, s_rows, norms, out):
    g_s = (total[...] + received[...]) * scale
    s_wide = s_rows[...].astype(jnp.float32)
    along = jnp.sum(s_wide * g_s, axis=1, keepdims=True)
    out[...] = (g_s - s_wide * along) / norms[:, :1]


def cost(rows, cols, width, bytes_accessed):
    return pl.CostEstimate(
        flops=8 * rows * cols * width, bytes_accessed=bytes_accessed, transcendentals=0
    )


def body(student, teacher):
    half, width = student.shape
    devices = lax.axis_size("blk")
    chips = devices // CORES
    rows = CORES * half
    text_count = half * devices
    bf16, f32 = jnp.bfloat16, jnp.float32
    vmem = pl.BlockSpec(memory_space=VMEM)
    anywhere = pl.BlockSpec(memory_space=pl.ANY)
    place = (lax.axis_index("blk") // CORES).reshape(1)

    def hop(value, shift, sources):
        pairs = [
            (CORES * i + c, CORES * (i + shift) + c) for i in sources for c in range(CORES)
        ]
        return lax.ppermute(value, "blk", pairs)

    def partner(value):
        return lax.ppermute(value, "blk", [(i, i ^ 1) for i in range(devices)])

    right, left, steps = (student, teacher), (student, teacher), []
    for step in range(1, chips):
        r_src, l_src = range(step - 1, chips - 1), range(1, chips - step + 1)
        s_pair = hop(right[0], 1, r_src), hop(left[0], -1, l_src)
        t_pair = hop(right[1], 1, r_src), hop(left[1], -1, l_src)
        right, left = (s_pair[0], t_pair[0]), (s_pair[1], t_pair[1])
        steps.append(right + left)

    s_other, t_other = partner(student), partner(teacher)
    s_rows, t_rows, norms, total = pl.pallas_call(
        first_kernel,
        out_shape=(
            jax.ShapeDtypeStruct((rows, width), bf16),
            jax.ShapeDtypeStruct((rows, width), bf16),
            jax.ShapeDtypeStruct((half, 128), f32),
            jax.ShapeDtypeStruct((rows, width), f32),
        ),
        in_specs=[vmem] * 4,
        out_specs=(vmem,) * 4,
        cost_estimate=cost(rows, half, width, 12 * rows * width),
    )(student, teacher, s_other, t_other)
    for step, blocks in enumerate(steps, 1):
        total = pl.pallas_call(
            functools.partial(step_kernel, step, chips - 1 - step),
            grid=(1,),
            out_shape=jax.ShapeDtypeStruct((rows, width), f32),
            in_specs=[pl.BlockSpec(memory_space=SMEM)] + [vmem] * 3 + [anywhere] * 4,
            out_specs=vmem,
            scratch_shapes=[pltpu.VMEM((half, width), bf16)] * 4
            + [pltpu.SemaphoreType.DMA((2,))],
            cost_estimate=cost(rows, 2 * half, width, 12 * rows * width),
        )(place, s_rows, t_rows, total, *blocks)
    received = partner(total[half:])
    return pl.pallas_call(
        functools.partial(last_kernel, width / text_count**0.5),
        grid=(1,),
        out_shape=jax.ShapeDtypeStruct((half, width), f32),
        in_specs=[
            pl.BlockSpec((half, width), lambda i: (0, 0)),
            pl.BlockSpec((half, width), lambda i: (0, 0)),
            pl.BlockSpec((half, width), lambda i: (0, 0)),
            pl.BlockSpec((half, 128), lambda i: (0, 0)),
        ],
        out_specs=pl.BlockSpec((half, width), lambda i: (0, 0)),
    )(total, received, s_rows, norms)


def solution(mesh):
    in_specs = (P(("grp", "blk"), None), P(("grp", "blk"), None))
    out_specs = P(("grp", "blk"), None)
    return jax.shard_map(body, mesh=mesh, in_specs=in_specs, out_specs=out_specs, check_vma=False)
```

time: 103 us -> 81.1 us (0.79); the launches traced: 103 us -> 79.9 us
  waiting for transfers between devices: 72.5 us -> 33 us
  Pallas kernels: 0 us -> 23.9 us
  starting transfers between devices: 0.04 us -> 19.8 us
  between operations: 13.4 us -> 0.31 us
  matrix products: 9.43 us -> 0 us
  other arithmetic: 7.21 us -> 0 us
  local copies, waits for them, and re-layouts: 0.2 us -> 2.87 us
    all_gather x2 -> x0, waiting for transfers between devices: 72.5 us -> none  [the longest x1 38 us: body(): s_piece = lax.all_gather(s_half, 'blk', axis=0, tiled=True)]
    ppermute x0 -> x15, waiting for transfers between devices: none -> 33 us  [the longest x12 30.7 us: hop(): return lax.ppermute(value, 'blk', pairs)]
    pallas_call x0 -> x5, Pallas kernels: none -> 23.9 us  [the longest x3 17 us: body(): pl.pallas_call(functools.partial(step_kernel, step, chips - 1 - step), gr...]
    ppermute x0 -> x15, starting transfers between devices: none -> 19.8 us  [the longest x12 19.6 us: hop(): return lax.ppermute(value, 'blk', pairs)]
    dot_general x4 -> x0, matrix products: 9.43 us -> none  [the longest x1 4.25 us: body(): lax.dot_general(s_half, s_piece, (((1,), (1,)), ((), ())), preferred_elem...]
    convert_element_type x2 -> x0, other arithmetic: 3.8 us -> none  [the longest x1 1.9 us: body(): s_half = s_float.astype(jnp.bfloat16)]
    reduce_sum x2 -> x0, other arithmetic: 2.31 us -> none  [normalize(): norms = jnp.sqrt(jnp.sum(floats * floats, axis=1, keepdims=True) + 1e-06)]
    unnamed x8 -> x22, local copies, waits for them, and re-layouts: 0.2 us -> 1.68 us
  transfers between devices with their start and end apart: 2 -> 15, of which waited for: 2 -> 6; matrix products, arithmetic and copies ran while one was open for 7% -> 0% of each run, Pallas kernels for 0% -> 19%
where the time goes in v1:
time: 81.1 us; the launch traced here: 79.9 us
  waiting for transfers between devices  33 us (41%)
  Pallas kernels  23.9 us (29%)
  starting transfers between devices  19.8 us (24%)
  local copies, waits for them, and re-layouts  2.87 us (4%)
    ppermute x12, waiting for transfers between devices, hop(): return lax.ppermute(value, 'blk', pairs)  30.7 us
    ppermute x12, starting transfers between devices, hop(): return lax.ppermute(value, 'blk', pairs)  19.6 us
    pallas_call x3, Pallas kernels, body(): pl.pallas_call(functools.partial(step_kernel, step, chips - 1 - step), gr...  17 us
    pallas_call x1, Pallas kernels, body(): pl.pallas_call(first_kernel, out_shape=(jax.ShapeDtypeStruct((rows, width...  4.19 us
    pallas_call x1, Pallas kernels, body(): pl.pallas_call(functools.partial(last_kernel, width / text_count ** 0.5),...  2.7 us
    ppermute x3, waiting for transfers between devices, partner(): return lax.ppermute(value, 'blk', [(i, i ^ 1) for i in range(devices)])  2.28 us
    unnamed x22, local copies, waits for them, and re-layouts  1.68 us
  transfers between devices with their start and end apart: 15, of which 6 were waited for; matrix products, arithmetic and copies ran while one was open for 0% of the time, Pallas kernels for 19%

profile of v1, /device:TPU:0, one launch (start us, length us, event | category | flops | bytes accessed | tf_op | source)
XLA Modules:
  0.0 79.9 jit_solution(8588788070190056089)
XLA Ops:
  0.0 5.0 %collective-permute-start.2 = (bf16[192,1024]{1,0:T(8,128)(2,1)}, bf16[192,1024]{1,0:T(8,128)(2,1)S(1)}, u32[]{:S(2)}, u32[]{:S(2)}) collective-permute-start(bf16[192,1024]{1,0:T(8,128)(2,1)} %s_own.1), channel_id=1, source_target_pairs={{0,2},{1,3},{2,4},{3,5},{4,6},{5,7},{8,10},{9,11},{10,12},{11,13},... | collective-permute-start | bytes 1179656 | tf_op jit(solution)/shard_map/ppermute | solution.py:117
  5.0 3.5 %collective-permute-start.3 = (bf16[192,1024]{1,0:T(8,128)(2,1)}, bf16[192,1024]{1,0:T(8,128)(2,1)S(1)}, u32[]{:S(2)}, u32[]{:S(2)}) collective-permute-start(bf16[192,1024]{1,0:T(8,128)(2,1)} %t_own.1), channel_id=1, source_target_pairs={{0,2},{1,3},{2,4},{3,5},{4,6},{5,7},{8,10},{9,11},{10,12},{11,13},... | collective-permute-start | bytes 1179656 | tf_op jit(solution)/shard_map/ppermute | solution.py:117
  8.5 1.3 %collective-permute-start.4 = (bf16[192,1024]{1,0:T(8,128)(2,1)}, bf16[192,1024]{1,0:T(8,128)(2,1)S(1)}, u32[]{:S(2)}, u32[]{:S(2)}) collective-permute-start(bf16[192,1024]{1,0:T(8,128)(2,1)} %s_own.1), channel_id=1, source_target_pairs={{2,0},{3,1},{4,2},{5,3},{6,4},{7,5},{10,8},{11,9},{12,10},{13,11},... | collective-permute-start | bytes 1179656 | tf_op jit(solution)/shard_map/ppermute | solution.py:117
  9.8 1.3 %collective-permute-start.5 = (bf16[192,1024]{1,0:T(8,128)(2,1)}, bf16[192,1024]{1,0:T(8,128)(2,1)S(1)}, u32[]{:S(2)}, u32[]{:S(2)}) collective-permute-start(bf16[192,1024]{1,0:T(8,128)(2,1)} %t_own.1), channel_id=1, source_target_pairs={{2,0},{3,1},{4,2},{5,3},{6,4},{7,5},{10,8},{11,9},{12,10},{13,11},... | collective-permute-start | bytes 1179656 | tf_op jit(solution)/shard_map/ppermute | solution.py:117
  11.1 3.6 %collective-permute-done.2.s_right = bf16[192,1024]{1,0:T(8,128)(2,1)S(1)} collective-permute-done((bf16[192,1024]{1,0:T(8,128)(2,1)}, bf16[192,1024]{1,0:T(8,128)(2,1)S(1)}, u32[]{:S(2)}, u32[]{:S(2)}) %collective-permute-start.2) | collective-permute-done | bytes 393248 | tf_op jit(solution)/shard_map/ppermute | solution.py:117
  15.4 6.6 %collective-permute-done.3.t_right = bf16[192,1024]{1,0:T(8,128)(2,1)S(1)} collective-permute-done((bf16[192,1024]{1,0:T(8,128)(2,1)}, bf16[192,1024]{1,0:T(8,128)(2,1)S(1)}, u32[]{:S(2)}, u32[]{:S(2)}) %collective-permute-start.3) | collective-permute-done | bytes 393248 | tf_op jit(solution)/shard_map/ppermute | solution.py:117
  22.8 1.3 %collective-permute-start.8 = (bf16[192,1024]{1,0:T(8,128)(2,1)S(1)}, bf16[192,1024]{1,0:T(8,128)(2,1)S(1)}, u32[]{:S(2)}, u32[]{:S(2)}) collective-permute-start(bf16[192,1024]{1,0:T(8,128)(2,1)S(1)} %collective-permute-done.4.s_left), channel_id=1, source_target_pairs={{2,0},{3,1},{4,2},{5,3},{10,8},{11,9},{12,10},{13,11},{18,16},{19,... | collective-permute-start | bytes 1179656 | tf_op jit(solution)/shard_map/ppermute | solution.py:117
  24.1 5.2 %collective-permute-done.5.t_left = bf16[192,1024]{1,0:T(8,128)(2,1)S(1)} collective-permute-done((bf16[192,1024]{1,0:T(8,128)(2,1)}, bf16[192,1024]{1,0:T(8,128)(2,1)S(1)}, u32[]{:S(2)}, u32[]{:S(2)}) %collective-permute-start.5) | collective-permute-done | bytes 393248 | tf_op jit(solution)/shard_map/ppermute | solution.py:117
  29.3 1.3 %collective-permute-start.9 = (bf16[192,1024]{1,0:T(8,128)(2,1)S(1)}, bf16[192,1024]{1,0:T(8,128)(2,1)S(1)}, u32[]{:S(2)}, u32[]{:S(2)}) collective-permute-start(bf16[192,1024]{1,0:T(8,128)(2,1)S(1)} %collective-permute-done.5.t_left), channel_id=1, source_target_pairs={{2,0},{3,1},{4,2},{5,3},{10,8},{11,9},{12,10},{13,11},{18,16},{19,... | collective-permute-start | bytes 1179656 | tf_op jit(solution)/shard_map/ppermute | solution.py:117
  30.7 0.7 collective-permute-start.10
  31.4 1.4 %collective-permute-start.11 = (bf16[192,1024]{1,0:T(8,128)(2,1)S(1)}, bf16[192,1024]{1,0:T(8,128)(2,1)}, u32[]{:S(2)}, u32[]{:S(2)}) collective-permute-start(bf16[192,1024]{1,0:T(8,128)(2,1)S(1)} %collective-permute-done.7.t_right), channel_id=1, source_target_pairs={{4,6},{5,7},{12,14},{13,15},{20,22},{21,23},{28,30},{29,31}} | collective-permute-start | bytes 1179656 | tf_op jit(solution)/shard_map/ppermute | solution.py:117
  32.8 8.1 %collective-permute-done.8.s_left = bf16[192,1024]{1,0:T(8,128)(2,1)S(1)} collective-permute-done((bf16[192,1024]{1,0:T(8,128)(2,1)S(1)}, bf16[192,1024]{1,0:T(8,128)(2,1)S(1)}, u32[]{:S(2)}, u32[]{:S(2)}) %collective-permute-start.8) | collective-permute-done | bytes 393248 | tf_op jit(solution)/shard_map/ppermute | solution.py:117
  40.9 1.3 %collective-permute-start.12 = (bf16[192,1024]{1,0:T(8,128)(2,1)S(1)}, bf16[192,1024]{1,0:T(8,128)(2,1)}, u32[]{:S(2)}, u32[]{:S(2)}) collective-permute-start(bf16[192,1024]{1,0:T(8,128)(2,1)S(1)} %collective-permute-done.8.s_left), channel_id=1, source_target_pairs={{2,0},{3,1},{10,8},{11,9},{18,16},{19,17},{26,24},{27,25}} | collective-permute-start | bytes 1179656 | tf_op jit(solution)/shard_map/ppermute | solution.py:117
  42.2 7.1 %collective-permute-done.9.t_left = bf16[192,1024]{1,0:T(8,128)(2,1)S(1)} collective-permute-done((bf16[192,1024]{1,0:T(8,128)(2,1)S(1)}, bf16[192,1024]{1,0:T(8,128)(2,1)S(1)}, u32[]{:S(2)}, u32[]{:S(2)}) %collective-permute-start.9) | collective-permute-done | bytes 393248 | tf_op jit(solution)/shard_map/ppermute | solution.py:117
  49.4 1.3 %collective-permute-start.13 = (bf16[192,1024]{1,0:T(8,128)(2,1)S(1)}, bf16[192,1024]{1,0:T(8,128)(2,1)}, u32[]{:S(2)}, u32[]{:S(2)}) collective-permute-start(bf16[192,1024]{1,0:T(8,128)(2,1)S(1)} %collective-permute-done.9.t_left), channel_id=1, source_target_pairs={{2,0},{3,1},{10,8},{11,9},{18,16},{19,17},{26,24},{27,25}} | collective-permute-start | bytes 1179656 | tf_op jit(solution)/shard_map/ppermute | solution.py:117
  50.7 4.2 %shard_map.28 = (bf16[384,1024]{1,0:T(8,128)(2,1)}, bf16[384,1024]{1,0:T(8,128)(2,1)}, f32[192,128]{1,0:T(8,128)}, f32[384,1024]{1,0:T(8,128)}) custom-call(bf16[192,1024]{1,0:T(8,128)(2,1)} %s_own.1, bf16[192,1024]{1,0:T(8,128)(2,1)} %t_own.1, bf16[192,1024]{1,0:T(8,128)(2,1)} %copy-done.10, bf16[192,1024]{1,0:T(8,128)(2,1)} %collective-permute-done.1.t_other), custom_call_target="tpu_custom_call" | custom-call | flops 603979776 | bytes 4718592 | tf_op jit(solution)/shard_map/pallas_call | solution.py:131
  54.9 5.7 %shard_map.29.total_in = f32[384,1024]{1,0:T(8,128)} custom-call(s32[1]{0:T(128)} %bitcast.place, bf16[384,1024]{1,0:T(8,128)(2,1)} %get-tuple-element.9.s_rows, bf16[384,1024]{1,0:T(8,128)(2,1)} %get-tuple-element.10.t_rows, f32[384,1024]{1,0:T(8,128)} %get-tuple-element.11.total_in, bf16[192,1024]{1,0:T(8,128)(2,1)} %copy-done.1, ...), custom_call_target="tpu_custom_call" | custom-call | flops 1207959552 | bytes 4718592 | tf_op jit(solution)/shard_map/pallas_call | solution.py:144
  60.6 5.7 %shard_map.30.total_in = f32[384,1024]{1,0:T(8,128)} custom-call(s32[1]{0:T(128)} %bitcast.place, bf16[384,1024]{1,0:T(8,128)(2,1)} %get-tuple-element.9.s_rows, bf16[384,1024]{1,0:T(8,128)(2,1)} %get-tuple-element.10.t_rows, f32[384,1024]{1,0:T(8,128)} %shard_map.29.total_in, bf16[192,1024]{1,0:T(8,128)(2,1)} %copy-done.5, bf16[192,1024]{1,0:T(8,128)(2,1)} %copy-done.6, ...), custom_call_target="tpu_custom_call" | custom-call | flops 1207959552 | bytes 4718592 | tf_op jit(solution)/shard_map/pallas_call | solution.py:144
  66.4 0.8 copy-done.9
  67.1 5.7 %shard_map.31.total = f32[384,1024]{1,0:T(8,128)} custom-call(s32[1]{0:T(128)} %bitcast.place, bf16[384,1024]{1,0:T(8,128)(2,1)} %get-tuple-element.9.s_rows, bf16[384,1024]{1,0:T(8,128)(2,1)} %get-tuple-element.10.t_rows, f32[384,1024]{1,0:T(8,128)} %shard_map.30.total_in, bf16[192,1024]{1,0:T(8,128)(2,1)} %copy-done.9, ...), custom_call_target="tpu_custom_call" | custom-call | flops 1207959552 | bytes 4718592 | tf_op jit(solution)/shard_map/pallas_call | solution.py:144
  72.8 1.2 %slice.4 = f32[192,1024]{1,0:T(8,128)S(1)} slice(f32[384,1024]{1,0:T(8,128)} %shard_map.31.total), slice={[192:384], [0:1024]} | slice | bytes 1572864 | tf_op jit(solution)/shard_map/slice | solution.py:154
  74.1 2.3 %collective-permute-done.14.received = f32[192,1024]{1,0:T(8,128)S(1)} collective-permute-done((f32[192,1024]{1,0:T(8,128)S(1)}, f32[192,1024]{1,0:T(8,128)S(1)}, u32[]{:S(2)}, u32[]{:S(2)}) %collective-permute-start.14) | collective-permute-done | bytes 786464 | tf_op jit(solution)/shard_map/ppermute | solution.py:120
  76.3 0.9 %copy-done = f32[192,1024]{1,0:T(8,128)} copy-done((f32[192,1024]{1,0:T(8,128)}, f32[192,1024]{1,0:T(8,128)S(1)}, u32[]{:S(2)}) %copy-start) | copy-done | bytes 786456
  77.2 2.7 %shard_map.32 = f32[192,1024]{1,0:T(8,128)} custom-call(f32[384,1024]{1,0:T(8,128)} %shard_map.31.total, f32[192,1024]{1,0:T(8,128)} %copy-done, bf16[384,1024]{1,0:T(8,128)(2,1)} %get-tuple-element.9.s_rows, f32[192,128]{1,0:T(8,128)} %get-tuple-element.12.norms), custom_call_target="tpu_custom_call" | custom-call | tf_op jit(solution)/shard_map/pallas_call | solution.py:155
  (34 shorter events, 1.6 us)
Async XLA Ops:
  0.0 14.8 %collective-permute-start.2 = (bf16[192,1024]{1,0:T(8,128)(2,1)}, bf16[192,1024]{1,0:T(8,128)(2,1)S(1)}, u32[]{:S(2)}, u32[]{:S(2)}) collective-permute-start(bf16[192,1024]{1,0:T(8,128)(2,1)} %s_own.1), channel_id=1, source_target_pairs={{0,2},{1,3},{2,4},{3,5},{4,6},{5,7},{8,10},{9,11},{10,12},{11,13},... | collective-permute-start | bytes 1179656 | tf_op jit(solution)/shard_map/ppermute | solution.py:117
  5.0 17.1 %collective-permute-start.3 = (bf16[192,1024]{1,0:T(8,128)(2,1)}, bf16[192,1024]{1,0:T(8,128)(2,1)S(1)}, u32[]{:S(2)}, u32[]{:S(2)}) collective-permute-start(bf16[192,1024]{1,0:T(8,128)(2,1)} %t_own.1), channel_id=1, source_target_pairs={{0,2},{1,3},{2,4},{3,5},{4,6},{5,7},{8,10},{9,11},{10,12},{11,13},... | collective-permute-start | bytes 1179656 | tf_op jit(solution)/shard_map/ppermute | solution.py:117
  8.5 14.3 %collective-permute-start.4 = (bf16[192,1024]{1,0:T(8,128)(2,1)}, bf16[192,1024]{1,0:T(8,128)(2,1)S(1)}, u32[]{:S(2)}, u32[]{:S(2)}) collective-permute-start(bf16[192,1024]{1,0:T(8,128)(2,1)} %s_own.1), channel_id=1, source_target_pairs={{2,0},{3,1},{4,2},{5,3},{6,4},{7,5},{10,8},{11,9},{12,10},{13,11},... | collective-permute-start | bytes 1179656 | tf_op jit(solution)/shard_map/ppermute | solution.py:117
  9.8 19.5 %collective-permute-start.5 = (bf16[192,1024]{1,0:T(8,128)(2,1)}, bf16[192,1024]{1,0:T(8,128)(2,1)S(1)}, u32[]{:S(2)}, u32[]{:S(2)}) collective-permute-start(bf16[192,1024]{1,0:T(8,128)(2,1)} %t_own.1), channel_id=1, source_target_pairs={{2,0},{3,1},{4,2},{5,3},{6,4},{7,5},{10,8},{11,9},{12,10},{13,11},... | collective-permute-start | bytes 1179656 | tf_op jit(solution)/shard_map/ppermute | solution.py:117
  11.1 19.5 %collective-permute-start = (bf16[192,1024]{1,0:T(8,128)(2,1)}, bf16[192,1024]{1,0:T(8,128)(2,1)S(1)}, u32[]{:S(2)}, u32[]{:S(2)}) collective-permute-start(bf16[192,1024]{1,0:T(8,128)(2,1)} %s_own.1), channel_id=1, source_target_pairs={{0,1},{1,0},{2,3},{3,2},{4,5},{5,4},{6,7},{7,6},{8,9},{9,8},{10,11... | collective-permute-start | bytes 1179656 | tf_op jit(solution)/shard_map/ppermute | solution.py:120
  14.8 40.1 %copy-start.1 = (bf16[192,1024]{1,0:T(8,128)(2,1)}, bf16[192,1024]{1,0:T(8,128)(2,1)S(1)}, u32[]{:S(2)}) copy-start(bf16[192,1024]{1,0:T(8,128)(2,1)S(1)} %collective-permute-done.2.s_right) | copy-start | bytes 1179652
  14.8 15.9 %collective-permute-start.6 = (bf16[192,1024]{1,0:T(8,128)(2,1)S(1)}, bf16[192,1024]{1,0:T(8,128)(2,1)S(1)}, u32[]{:S(2)}, u32[]{:S(2)}) collective-permute-start(bf16[192,1024]{1,0:T(8,128)(2,1)S(1)} %collective-permute-done.2.s_right), channel_id=1, source_target_pairs={{2,4},{3,5},{4,6},{5,7},{10,12},{11,13},{12,14},{13,15},{18,20},{1... | collective-permute-start | bytes 1179656 | tf_op jit(solution)/shard_map/ppermute | solution.py:117
  22.1 32.8 %copy-start.2 = (bf16[192,1024]{1,0:T(8,128)(2,1)}, bf16[192,1024]{1,0:T(8,128)(2,1)S(1)}, u32[]{:S(2)}) copy-start(bf16[192,1024]{1,0:T(8,128)(2,1)S(1)} %collective-permute-done.3.t_right) | copy-start | bytes 1179652
  22.1 9.3 %collective-permute-start.7 = (bf16[192,1024]{1,0:T(8,128)(2,1)S(1)}, bf16[192,1024]{1,0:T(8,128)(2,1)S(1)}, u32[]{:S(2)}, u32[]{:S(2)}) collective-permute-start(bf16[192,1024]{1,0:T(8,128)(2,1)S(1)} %collective-permute-done.3.t_right), channel_id=1, source_target_pairs={{2,4},{3,5},{4,6},{5,7},{10,12},{11,13},{12,14},{13,15},{18,20},{1... | collective-permute-start | bytes 1179656 | tf_op jit(solution)/shard_map/ppermute | solution.py:117
  22.7 32.1 %copy-start.3 = (bf16[192,1024]{1,0:T(8,128)(2,1)}, bf16[192,1024]{1,0:T(8,128)(2,1)S(1)}, u32[]{:S(2)}) copy-start(bf16[192,1024]{1,0:T(8,128)(2,1)S(1)} %collective-permute-done.4.s_left) | copy-start | bytes 1179652
  22.8 18.2 %collective-permute-start.8 = (bf16[192,1024]{1,0:T(8,128)(2,1)S(1)}, bf16[192,1024]{1,0:T(8,128)(2,1)S(1)}, u32[]{:S(2)}, u32[]{:S(2)}) collective-permute-start(bf16[192,1024]{1,0:T(8,128)(2,1)S(1)} %collective-permute-done.4.s_left), channel_id=1, source_target_pairs={{2,0},{3,1},{4,2},{5,3},{10,8},{11,9},{12,10},{13,11},{18,16},{19,... | collective-permute-start | bytes 1179656 | tf_op jit(solution)/shard_map/ppermute | solution.py:117
  29.3 25.6 %copy-start.4 = (bf16[192,1024]{1,0:T(8,128)(2,1)}, bf16[192,1024]{1,0:T(8,128)(2,1)S(1)}, u32[]{:S(2)}) copy-start(bf16[192,1024]{1,0:T(8,128)(2,1)S(1)} %collective-permute-done.5.t_left) | copy-start | bytes 1179652
  29.3 20.1 %collective-permute-start.9 = (bf16[192,1024]{1,0:T(8,128)(2,1)S(1)}, bf16[192,1024]{1,0:T(8,128)(2,1)S(1)}, u32[]{:S(2)}, u32[]{:S(2)}) collective-permute-start(bf16[192,1024]{1,0:T(8,128)(2,1)S(1)} %collective-permute-done.5.t_left), channel_id=1, source_target_pairs={{2,0},{3,1},{4,2},{5,3},{10,8},{11,9},{12,10},{13,11},{18,16},{19,... | collective-permute-start | bytes 1179656 | tf_op jit(solution)/shard_map/ppermute | solution.py:117
  30.6 18.8 %copy-start.10 = (bf16[192,1024]{1,0:T(8,128)(2,1)}, bf16[192,1024]{1,0:T(8,128)(2,1)S(1)}, u32[]{:S(2)}) copy-start(bf16[192,1024]{1,0:T(8,128)(2,1)S(1)} %collective-permute-done.s_other) | copy-start | bytes 1179652
  30.6 20.1 %collective-permute-start.1 = (bf16[192,1024]{1,0:T(8,128)(2,1)}, bf16[192,1024]{1,0:T(8,128)(2,1)}, u32[]{:S(2)}, u32[]{:S(2)}) collective-permute-start(bf16[192,1024]{1,0:T(8,128)(2,1)} %t_own.1), channel_id=1, source_target_pairs={{0,1},{1,0},{2,3},{3,2},{4,5},{5,4},{6,7},{7,6},{8,9},{9,8},{10,11... | collective-permute-start | bytes 1179656 | tf_op jit(solution)/shard_map/ppermute | solution.py:120
  30.7 29.9 %copy-start.5 = (bf16[192,1024]{1,0:T(8,128)(2,1)}, bf16[192,1024]{1,0:T(8,128)(2,1)S(1)}, u32[]{:S(2)}) copy-start(bf16[192,1024]{1,0:T(8,128)(2,1)S(1)} %collective-permute-done.6.s_right) | copy-start | bytes 1179652
  30.7 35.6 %collective-permute-start.10 = (bf16[192,1024]{1,0:T(8,128)(2,1)S(1)}, bf16[192,1024]{1,0:T(8,128)(2,1)S(1)}, u32[]{:S(2)}, u32[]{:S(2)}) collective-permute-start(bf16[192,1024]{1,0:T(8,128)(2,1)S(1)} %collective-permute-done.6.s_right), channel_id=1, source_target_pairs={{4,6},{5,7},{12,14},{13,15},{20,22},{21,23},{28,30},{29,31}} | collective-permute-start | bytes 1179656 | tf_op jit(solution)/shard_map/ppermute | solution.py:117
  31.4 29.2 %copy-start.6 = (bf16[192,1024]{1,0:T(8,128)(2,1)}, bf16[192,1024]{1,0:T(8,128)(2,1)S(1)}, u32[]{:S(2)}) copy-start(bf16[192,1024]{1,0:T(8,128)(2,1)S(1)} %collective-permute-done.7.t_right) | copy-start | bytes 1179652
  31.4 34.9 %collective-permute-start.11 = (bf16[192,1024]{1,0:T(8,128)(2,1)S(1)}, bf16[192,1024]{1,0:T(8,128)(2,1)}, u32[]{:S(2)}, u32[]{:S(2)}) collective-permute-start(bf16[192,1024]{1,0:T(8,128)(2,1)S(1)} %collective-permute-done.7.t_right), channel_id=1, source_target_pairs={{4,6},{5,7},{12,14},{13,15},{20,22},{21,23},{28,30},{29,31}} | collective-permute-start | bytes 1179656 | tf_op jit(solution)/shard_map/ppermute | solution.py:117
  40.9 19.6 %copy-start.7 = (bf16[192,1024]{1,0:T(8,128)(2,1)}, bf16[192,1024]{1,0:T(8,128)(2,1)S(1)}, u32[]{:S(2)}) copy-start(bf16[192,1024]{1,0:T(8,128)(2,1)S(1)} %collective-permute-done.8.s_left) | copy-start | bytes 1179652
  40.9 25.4 %collective-permute-start.12 = (bf16[192,1024]{1,0:T(8,128)(2,1)S(1)}, bf16[192,1024]{1,0:T(8,128)(2,1)}, u32[]{:S(2)}, u32[]{:S(2)}) collective-permute-start(bf16[192,1024]{1,0:T(8,128)(2,1)S(1)} %collective-permute-done.8.s_left), channel_id=1, source_target_pairs={{2,0},{3,1},{10,8},{11,9},{18,16},{19,17},{26,24},{27,25}} | collective-permute-start | bytes 1179656 | tf_op jit(solution)/shard_map/ppermute | solution.py:117
  49.4 11.2 %copy-start.8 = (bf16[192,1024]{1,0:T(8,128)(2,1)}, bf16[192,1024]{1,0:T(8,128)(2,1)S(1)}, u32[]{:S(2)}) copy-start(bf16[192,1024]{1,0:T(8,128)(2,1)S(1)} %collective-permute-done.9.t_left) | copy-start | bytes 1179652
  49.4 17.0 %collective-permute-start.13 = (bf16[192,1024]{1,0:T(8,128)(2,1)S(1)}, bf16[192,1024]{1,0:T(8,128)(2,1)}, u32[]{:S(2)}, u32[]{:S(2)}) collective-permute-start(bf16[192,1024]{1,0:T(8,128)(2,1)S(1)} %collective-permute-done.9.t_left), channel_id=1, source_target_pairs={{2,0},{3,1},{10,8},{11,9},{18,16},{19,17},{26,24},{27,25}} | collective-permute-start | bytes 1179656 | tf_op jit(solution)/shard_map/ppermute | solution.py:117
  74.0 2.4 %collective-permute-start.14 = (f32[192,1024]{1,0:T(8,128)S(1)}, f32[192,1024]{1,0:T(8,128)S(1)}, u32[]{:S(2)}, u32[]{:S(2)}) collective-permute-start(f32[192,1024]{1,0:T(8,128)S(1)} %slice.4), channel_id=1, source_target_pairs={{0,1},{1,0},{2,3},{3,2},{4,5},{5,4},{6,7},{7,6},{8,9},{9,8},{10,11... | collective-permute-start | bytes 2359304 | tf_op jit(solution)/shard_map/ppermute | solution.py:120
  (2 other events, 1.7 us)

commit v2 on v0

v2 whole, which is shorter than its diff:
```python
import functools

import jax
import jax.numpy as jnp
from jax import lax
from jax.experimental import pallas as pl
from jax.experimental.pallas import tpu as pltpu
from jax.sharding import PartitionSpec as P


CORES = 2
VMEM = pltpu.MemorySpace.VMEM
SMEM = pltpu.MemorySpace.SMEM
NT = (((1,), (1,)), ((), ()))
TN = (((0,), (0,)), ((), ()))
GRANT = 16 * 2**20


def dot(left, right, dims=(((1,), (0,)), ((), ()))):
    return lax.dot_general(left, right, dims, preferred_element_type=jnp.float32)


def normalized(ref):
    floats = ref[...].astype(jnp.float32)
    norms = jnp.sqrt(jnp.sum(floats * floats, axis=1, keepdims=True) + 1e-06)
    return (floats / norms).astype(jnp.bfloat16), norms


def gram(s_rows, t_rows, s_cols, t_cols):
    return dot(s_rows, s_cols, NT) - dot(t_rows, t_cols, NT)


def accumulate(s_rows, t_rows, s_cols, t_cols, totals, fresh=False):
    half = s_cols.shape[0]
    for index, total in enumerate(totals):
        rows = pl.ds(index * half, half)
        block = gram(s_rows[rows, :], t_rows[rows, :], s_cols[...], t_cols[...])
        high = block.astype(jnp.bfloat16)
        low = (block - high.astype(jnp.float32)).astype(jnp.bfloat16)
        product = dot(high, s_cols[...]) + dot(low, s_cols[...])
        total[...] = product if fresh else total[...] + product


def normalize_pair(first, second, out):
    half = first.shape[0]
    out[pl.ds(0, half), :], norm = normalized(first)
    out[pl.ds(half, half), :], _ = normalized(second)
    return norm


def first_kernel(s_own, t_own, s_other, t_other, s_rows, t_rows, norms, mine, theirs):
    own = pl.ds(0, s_own.shape[0])
    norm = normalize_pair(s_own, s_other, s_rows)
    norms[...] = jnp.broadcast_to(norm, norms.shape)
    normalize_pair(t_own, t_other, t_rows)
    accumulate(
        s_rows, t_rows, s_rows.at[own, :], t_rows.at[own, :], (mine, theirs), fresh=True
    )


def end_rows_kernel(s_own, t_own, s_other, t_other, s_end, t_end):
    normalize_pair(s_own, s_other, s_end)
    normalize_pair(t_own, t_other, t_end)


def end_block_kernel(next_to_end, s_end, t_end, s_block, t_block, e_out):
    @pl.when(next_to_end[0] > 0)
    def _():
        s_cols, _ = normalized(s_block)
        t_cols, _ = normalized(t_block)
        e_out[...] = gram(s_cols, t_cols, s_end[...], t_end[...]).astype(e_out.dtype)


def last_block_kernel(next_to_end, s_end, t_end, s_block, t_block, same, cross):
    @pl.when(next_to_end[0] > 0)
    def _():
        half = s_block.shape[0]
        s_cols, _ = normalized(s_block)
        t_cols, _ = normalized(t_block)
        for index, out in enumerate((same, cross)):
            rows = pl.ds(index * half, half)
            block = gram(s_end[rows, :], t_end[rows, :], s_cols, t_cols)
            out[...] = block.astype(out.dtype)


def step_kernel(kinds, oks, s_rows, t_rows, mine_in, theirs_in, *refs):
    half = mine_in.shape[0]
    blocks, (mine, theirs, s_cols, t_cols) = refs[:-4], refs[-4:]
    for index, ready in enumerate(kinds):
        s_block, other = blocks[2 * index], blocks[2 * index + 1]

        @pl.when(oks[index] > 0)
        def _(s_block=s_block, other=other, ready=ready):
            s_cols[...], _ = normalized(s_block)
            if ready:
                for place, total in enumerate((mine, theirs)):
                    part = other[:, place * half : (place + 1) * half]
                    total[...] += dot(part, s_cols[...], TN)
            else:
                t_cols[...], _ = normalized(other)
                accumulate(s_rows, t_rows, s_cols, t_cols, (mine, theirs))


def sum_kernel(at_end, mine, received, s_near, s_far, total, s_last):
    total[...] = mine[...] + received[...]

    @pl.when(at_end[0] > 0)
    def _():
        normalize_pair(s_near, s_far, s_last)


def last_kernel(scale, at_end, total, s_rows, norms, s_last, same, cross, out, g_s):
    half = total.shape[0]
    g_s[...] = total[...]

    @pl.when(at_end[0] > 0)
    def _():
        g_s[...] += dot(same[...], s_last[pl.ds(0, half), :]) + dot(
            cross[...], s_last[pl.ds(half, half), :]
        )

    scaled = g_s[...] * scale
    s_wide = s_rows[pl.ds(0, half), :].astype(jnp.float32)
    along = jnp.sum(s_wide * scaled, axis=1, keepdims=True)
    out[...] = (scaled - s_wide * along) / norms[:, :1]


def cost(rows, cols, width):
    return pl.CostEstimate(
        flops=8 * rows * cols * width, bytes_accessed=8 * rows * width, transcendentals=0
    )


def body(student, teacher):
    half, width = student.shape
    devices = lax.axis_size("blk")
    chips = devices // CORES
    rows = CORES * half
    text_count = half * devices
    bf16, f32 = jnp.bfloat16, jnp.float32
    shape = jax.ShapeDtypeStruct
    vmem = pl.BlockSpec(memory_space=VMEM)
    smem = pl.BlockSpec(memory_space=SMEM)
    chip = lax.div(lax.axis_index("blk"), CORES)
    flag = lambda value: value.astype(jnp.int32).reshape(1)
    at_end = (chip == 0) | (chip == chips - 1)
    next_to_end = flag((chip == 1) | (chip == chips - 2))
    at_end = flag(at_end)
    ends = (0, chips - 1)

    def call(kernel, outs, *args, flags=0, cols=half, **options):
        return run(kernel, outs, *args, flags=flags, cols=cols, **options)

    def run(kernel, outs, *args, flags, cols, **options):
        return pl.pallas_call(
            kernel,
            out_shape=outs,
            in_specs=[smem] * flags + [vmem] * (len(args) - flags),
            out_specs=jax.tree.map(lambda _: vmem, outs),
            compiler_params=pltpu.CompilerParams(vmem_limit_bytes=GRANT),
            cost_estimate=cost(rows, cols, width),
            **options,
        )(*args)

    def permute(value, pairs, cross=0):
        cores = [(CORES * a + c, CORES * b + (c ^ cross)) for a, b in pairs for c in range(CORES)]
        return lax.ppermute(value, "blk", cores)

    def partner(value, among=range(chips)):
        return permute(value, [(i, i) for i in among], cross=1)

    def links(step, parity):
        for low in range(parity, chips - 1, 2):
            if low - step + 1 >= 0:
                yield low, low + 1
            if low + step <= chips - 1:
                yield low + 1, low

    inner = [i for i in (1, chips - 2)]
    s_rows, t_rows, norms, mine, theirs = call(
        first_kernel,
        (
            shape((rows, width), bf16),
            shape((rows, width), bf16),
            shape((half, 128), f32),
            shape((half, width), f32),
            shape((half, width), f32),
        ),
        student,
        teacher,
        partner(student),
        partner(teacher),
    )

    held = ((student, teacher),) * 2
    e_block = None
    for step in range(1, chips - 1):
        moved, kinds, oks, blocks = [], [], [], []
        for parity in range(2):
            moves = list(links(step, parity))
            before = held[1 - parity]
            through = [m for m in moves if step == 1 or m[1] not in ends]
            s_block = permute(before[0], moves) if moves else None
            t_block = permute(before[1], through) if through else None
            moved.append((s_block, t_block))
            up = lax.rem(chip, 2) == parity
            here = jnp.where(up, chip + step <= chips - 1, chip >= step)
            if through:
                kinds.append(False)
                oks.append(here & (at_end[0] == 0) if step > 1 else here)
                blocks.extend((s_block, t_block))
            if len(through) < len(moves):
                kinds.append(True)
                oks.append(here & (at_end[0] > 0))
                e_here = permute(e_block, [m for m in moves if m[1] in ends])
                blocks.extend((s_block, e_here))
        held = tuple(moved)
        if step == 1:
            first = held[0]
            s_end, t_end = call(
                end_rows_kernel,
                (shape((rows, width), bf16),) * 2,
                *first,
                partner(first[0], inner),
                partner(first[1], inner),
            )
        if step < chips - 2:
            e_block = call(
                end_block_kernel,
                shape((half, rows), bf16),
                next_to_end, s_end, t_end, *held[1],
                flags=1,
            )
        else:
            same, cross = call(
                last_block_kernel,
                (shape((half, half), bf16),) * 2,
                next_to_end, s_end, t_end, *held[1],
                flags=1,
            )
        mine, theirs = call(
            functools.partial(step_kernel, tuple(kinds)),
            (shape((half, width), f32),) * 2,
            jnp.stack(oks).astype(jnp.int32), s_rows, t_rows, mine, theirs, *blocks,
            flags=1,
            input_output_aliases={3: 0, 4: 1},
            scratch_shapes=[pltpu.VMEM((half, width), bf16)] * 2,
        )
    last = [(1, 0), (chips - 2, chips - 1)]
    s_last = permute(held[1][0], last)
    same = permute(same, last)
    cross = permute(cross, last, cross=1)
    total, s_last = call(
        sum_kernel,
        (shape((half, width), f32), shape((rows, width), bf16)),
        at_end, mine, partner(theirs), s_last, partner(s_last, ends),
        flags=1,
    )
    return call(
        functools.partial(last_kernel, width / text_count**0.5),
        shape((half, width), f32),
        at_end, total, s_rows, norms, s_last, same, cross,
        flags=1,
        scratch_shapes=[pltpu.VMEM((half, width), f32)],
    )


def solution(mesh):
    rows = P(("grp", "blk"), None)
    return jax.shard_map(
        body, mesh=mesh, in_specs=(rows, rows), out_specs=rows, check_vma=False
    )
```

time: 103 us -> 67.1 us (0.65)
  waiting for transfers between devices: 72.5 us -> 39.3 us
  starting transfers between devices: 0.04 us -> 16.3 us
  between operations: 13.4 us -> 0.27 us
  matrix products: 9.43 us -> 0 us
  Pallas kernels: 0 us -> 7.27 us
  other arithmetic: 7.21 us -> 0.15 us
  local copies, waits for them, and re-layouts: 0.2 us -> 3.49 us
    all_gather x2 -> x0, waiting for transfers between devices: 72.5 us -> none  [the longest x1 38 us: body(): s_piece = lax.all_gather(s_half, 'blk', axis=0, tiled=True)]
    ppermute x0 -> x17, waiting for transfers between devices: none -> 39.3 us  [permute(): return lax.ppermute(value, 'blk', cores)]
    ppermute x0 -> x17, starting transfers between devices: none -> 16.3 us  [permute(): return lax.ppermute(value, 'blk', cores)]
    dot_general x4 -> x0, matrix products: 9.43 us -> none  [the longest x1 4.25 us: body(): lax.dot_general(s_half, s_piece, (((1,), (1,)), ((), ())), preferred_elem...]
    pallas_call x0 -> x8, Pallas kernels: none -> 7.27 us  [run(): pl.pallas_call(kernel, out_shape=outs, in_specs=[smem] * flags + [vmem] *...]
    convert_element_type x2, other arithmetic: 3.8 us -> 0.15 us  [body(): jnp.stack(oks).astype(jnp.int32)]
    unnamed x8 -> x12, local copies, waits for them, and re-layouts: 0.2 us -> 3.49 us
    reduce_sum x2 -> x0, other arithmetic: 2.31 us -> none  [normalize(): norms = jnp.sqrt(jnp.sum(floats * floats, axis=1, keepdims=True) + 1e-06)]
  transfers between devices with their start and end apart: 2 -> 17, of which waited for: 2 -> 7; matrix products, arithmetic and copies ran while one was open for 7% -> 0% of each run, Pallas kernels for 0% -> 9%
where the time goes in v2:
time: 67.1 us; the launch traced here: 66.7 us
  waiting for transfers between devices  39.3 us (59%)
  starting transfers between devices  16.3 us (24%)
  Pallas kernels  7.27 us (11%)
  local copies, waits for them, and re-layouts  3.49 us (5%)
    ppermute x17, waiting for transfers between devices, permute(): return lax.ppermute(value, 'blk', cores)  39.3 us
    ppermute x17, starting transfers between devices, permute(): return lax.ppermute(value, 'blk', cores)  16.3 us
    pallas_call x8, Pallas kernels, run(): pl.pallas_call(kernel, out_shape=outs, in_specs=[smem] * flags + [vmem] *...  7.27 us
    unnamed x12, local copies, waits for them, and re-layouts  3.49 us
  transfers between devices with their start and end apart: 17, of which 7 were waited for; matrix products, arithmetic and copies ran while one was open for 0% of the time, Pallas kernels for 9%

profile of v2, /device:TPU:0, one launch (start us, length us, event | category | flops | bytes accessed | tf_op | source)
XLA Modules:
  0.0 66.7 jit_solution(16760405677280401300)
XLA Ops:
  0.0 3.1 %collective-permute-start.2 = (bf16[192,1024]{1,0:T(8,128)(2,1)}, bf16[192,1024]{1,0:T(8,128)(2,1)S(1)}, u32[]{:S(2)}, u32[]{:S(2)}) collective-permute-start(bf16[192,1024]{1,0:T(8,128)(2,1)} %s_own.1), channel_id=1, source_target_pairs={{0,2},{1,3},{2,0},{3,1},{4,6},{5,7},{6,4},{7,5},{8,10},{9,11},{10,... | collective-permute-start | bytes 1179656 | tf_op jit(solution)/shard_map/ppermute | solution.py:167
  3.8 0.7 %collective-permute-start.5 = (bf16[192,1024]{1,0:T(8,128)(2,1)}, bf16[192,1024]{1,0:T(8,128)(2,1)S(1)}, u32[]{:S(2)}, u32[]{:S(2)}) collective-permute-start(bf16[192,1024]{1,0:T(8,128)(2,1)} %t_own.1), channel_id=1, source_target_pairs={{2,4},{3,5},{4,2},{5,3},{10,12},{11,13},{12,10},{13,11},{18,20},{1... | collective-permute-start | bytes 1179656 | tf_op jit(solution)/shard_map/ppermute | solution.py:167
  4.5 8.8 %collective-permute-done.2.refs_0_.s_own = bf16[192,1024]{1,0:T(8,128)(2,1)S(1)} collective-permute-done((bf16[192,1024]{1,0:T(8,128)(2,1)}, bf16[192,1024]{1,0:T(8,128)(2,1)S(1)}, u32[]{:S(2)}, u32[]{:S(2)}) %collective-permute-start.2) | collective-permute-done | bytes 393248 | tf_op jit(solution)/shard_map/ppermute | solution.py:167
  13.9 6.9 %collective-permute-done.3.refs_1_.t_own = bf16[192,1024]{1,0:T(8,128)(2,1)S(1)} collective-permute-done((bf16[192,1024]{1,0:T(8,128)(2,1)}, bf16[192,1024]{1,0:T(8,128)(2,1)S(1)}, u32[]{:S(2)}, u32[]{:S(2)}) %collective-permute-start.3) | collective-permute-done | bytes 393248 | tf_op jit(solution)/shard_map/ppermute | solution.py:167
  22.1 0.7 %collective-permute-start.10 = (bf16[192,1024]{1,0:T(8,128)(2,1)S(1)}, bf16[192,1024]{1,0:T(8,128)(2,1)S(1)}, u32[]{:S(2)}, u32[]{:S(2)}) collective-permute-start(bf16[192,1024]{1,0:T(8,128)(2,1)S(1)} %collective-permute-done.2.refs_0_.s_own), channel_id=1, source_target_pairs={{2,4},{3,5},{4,2},{5,3},{10,12},{11,13},{12,10},{13,11},{18,20},{1... | collective-permute-start | bytes 1179656 | tf_op jit(solution)/shard_map/ppermute | solution.py:167
  22.8 0.7 %copy-done.2 = bf16[192,1024]{1,0:T(8,128)(2,1)} copy-done((bf16[192,1024]{1,0:T(8,128)(2,1)}, bf16[192,1024]{1,0:T(8,128)(2,1)S(1)}, u32[]{:S(2)}) %copy-start.2) | copy-done | bytes 393240
  24.2 0.7 %copy-done.4 = bf16[192,1024]{1,0:T(8,128)(2,1)} copy-done((bf16[192,1024]{1,0:T(8,128)(2,1)}, bf16[192,1024]{1,0:T(8,128)(2,1)S(1)}, u32[]{:S(2)}) %copy-start.4) | copy-done | bytes 393240
  25.0 1.3 %collective-permute-start.6 = (bf16[192,1024]{1,0:T(8,128)(2,1)S(1)}, bf16[192,1024]{1,0:T(8,128)(2,1)S(1)}, u32[]{:S(2)}, u32[]{:S(2)}) collective-permute-start(bf16[192,1024]{1,0:T(8,128)(2,1)S(1)} %collective-permute-done.4.refs_2_.s_block), channel_id=1, source_target_pairs={{2,0},{3,1},{4,6},{5,7},{10,8},{11,9},{12,14},{13,15},{18,16},{19,... | collective-permute-start | bytes 1179656 | tf_op jit(solution)/shard_map/ppermute | solution.py:167
  26.3 1.0 %copy-done.3 = bf16[192,1024]{1,0:T(8,128)(2,1)S(1)} copy-done((bf16[192,1024]{1,0:T(8,128)(2,1)S(1)}, bf16[192,1024]{1,0:T(8,128)(2,1)}, u32[]{:S(2)}) %copy-start.3) | copy-done | bytes 393240
  27.3 1.0 %copy-done.5 = bf16[192,1024]{1,0:T(8,128)(2,1)S(1)} copy-done((bf16[192,1024]{1,0:T(8,128)(2,1)S(1)}, bf16[192,1024]{1,0:T(8,128)(2,1)}, u32[]{:S(2)}) %copy-start.5) | copy-done | bytes 393240
  29.0 1.4 %collective-permute-start.9 = (bf16[192,384]{1,0:T(8,128)(2,1)S(1)}, bf16[192,384]{1,0:T(8,128)(2,1)S(1)}, u32[]{:S(2)}, u32[]{:S(2)}) collective-permute-start(bf16[192,384]{1,0:T(8,128)(2,1)S(1)} %shard_map.31), channel_id=1, source_target_pairs={{2,0},{3,1},{4,6},{5,7},{10,8},{11,9},{12,14},{13,15},{18,16},{19,... | collective-permute-start | bytes 442376 | tf_op jit(solution)/shard_map/ppermute | solution.py:167
  30.5 1.6 %shard_map.28 = (bf16[384,1024]{1,0:T(8,128)(2,1)S(1)}, bf16[384,1024]{1,0:T(8,128)(2,1)S(1)}, f32[192,128]{1,0:T(8,128)S(1)}, f32[192,1024]{1,0:T(8,128)S(1)}, f32[192,1024]{1,0:T(8,128)S(1)}) custom-call(bf16[192,1024]{1,0:T(8,128)(2,1)S(1)} %copy-done, bf16[192,1024]{1,0:T(8,128)(2,1)S(1)} %copy-done.1, ...), custom_call_target="tpu_custom_call" | custom-call | flops 603979776 | bytes 3145728 | tf_op jit(solution)/shard_map/pallas_call | solution.py:155
  32.1 2.0 %shard_map.29 = (f32[192,1024]{1,0:T(8,128)S(1)}, f32[192,1024]{1,0:T(8,128)S(1)}) custom-call(s32[2]{0:T(128)S(1)} %add_convert_fusion.1.oks, bf16[384,1024]{1,0:T(8,128)(2,1)S(1)} %get-tuple-element.20.s_rows, bf16[384,1024]{1,0:T(8,128)(2,1)S(1)} %get-tuple-element.21.t_rows, ...), custom_call_target="tpu_custom_call", output_to_operand_aliasing={{0}: (3, {}), {1}: (4, {})} | custom-call | flops 603979776 | bytes 3145728 | tf_op jit(solution)/shard_map/pallas_call | solution.py:155
  34.1 1.3 %collective-permute-start.13 = (bf16[192,1024]{1,0:T(8,128)(2,1)S(1)}, bf16[192,1024]{1,0:T(8,128)(2,1)S(1)}, u32[]{:S(2)}, u32[]{:S(2)}) collective-permute-start(bf16[192,1024]{1,0:T(8,128)(2,1)S(1)} %collective-permute-done.10.refs_2_.s_block), channel_id=1, source_target_pairs={{2,0},{3,1},{4,6},{5,7},{10,8},{11,9},{12,14},{13,15},{18,16},{19,... | collective-permute-start | bytes 1179656 | tf_op jit(solution)/shard_map/ppermute | solution.py:167
  35.4 9.0 %collective-permute-done.6.refs_0_ = bf16[192,1024]{1,0:T(8,128)(2,1)S(1)} collective-permute-done((bf16[192,1024]{1,0:T(8,128)(2,1)S(1)}, bf16[192,1024]{1,0:T(8,128)(2,1)S(1)}, u32[]{:S(2)}, u32[]{:S(2)}) %collective-permute-start.6) | collective-permute-done | bytes 393248 | tf_op jit(solution)/shard_map/ppermute | solution.py:167
  44.5 1.9 %collective-permute-done.9.refs_1_ = bf16[192,384]{1,0:T(8,128)(2,1)S(1)} collective-permute-done((bf16[192,384]{1,0:T(8,128)(2,1)S(1)}, bf16[192,384]{1,0:T(8,128)(2,1)S(1)}, u32[]{:S(2)}, u32[]{:S(2)}) %collective-permute-start.9) | collective-permute-done | bytes 147488 | tf_op jit(solution)/shard_map/ppermute | solution.py:167
  46.4 1.1 %shard_map.32 = (f32[192,1024]{1,0:T(8,128)S(1)}, f32[192,1024]{1,0:T(8,128)S(1)}) custom-call(s32[2]{0:T(128)S(1)} %add_convert_fusion.oks, bf16[384,1024]{1,0:T(8,128)(2,1)S(1)} %get-tuple-element.20.s_rows, bf16[384,1024]{1,0:T(8,128)(2,1)S(1)} %get-tuple-element.21.t_rows, ...), custom_call_target="tpu_custom_call", output_to_operand_aliasing={{0}: (3, {}), {1}: (4, {})} | custom-call | flops 603979776 | bytes 3145728 | tf_op jit(solution)/shard_map/pallas_call | solution.py:155
  47.5 6.9 %collective-permute-done.13.s_near = bf16[192,1024]{1,0:T(8,128)(2,1)S(1)} collective-permute-done((bf16[192,1024]{1,0:T(8,128)(2,1)S(1)}, bf16[192,1024]{1,0:T(8,128)(2,1)S(1)}, u32[]{:S(2)}, u32[]{:S(2)}) %collective-permute-start.13) | collective-permute-done | bytes 393248 | tf_op jit(solution)/shard_map/ppermute | solution.py:167
  54.5 1.9 %collective-permute-start.14 = (bf16[192,1024]{1,0:T(8,128)(2,1)S(1)}, bf16[192,1024]{1,0:T(8,128)(2,1)S(1)}, u32[]{:S(2)}, u32[]{:S(2)}) collective-permute-start(bf16[192,1024]{1,0:T(8,128)(2,1)S(1)} %collective-permute-done.13.s_near), channel_id=1, source_target_pairs={{0,1},{1,0},{6,7},{7,6},{8,9},{9,8},{14,15},{15,14},{16,17},{17,16... | collective-permute-start | bytes 1179656 | tf_op jit(solution)/shard_map/ppermute | solution.py:167
  56.4 1.3 %collective-permute-start.15 = (bf16[192,192]{1,0:T(8,128)(2,1)S(1)}, bf16[192,192]{1,0:T(8,128)(2,1)S(1)}, u32[]{:S(2)}, u32[]{:S(2)}) collective-permute-start(bf16[192,192]{1,0:T(8,128)(2,1)S(1)} %get-tuple-element.33), channel_id=1, source_target_pairs={{2,0},{3,1},{4,6},{5,7},{10,8},{11,9},{12,14},{13,15},{18,16},{19,... | collective-permute-start | bytes 221192 | tf_op jit(solution)/shard_map/ppermute | solution.py:167
  57.7 1.3 %collective-permute-start.16 = (bf16[192,192]{1,0:T(8,128)(2,1)S(1)}, bf16[192,192]{1,0:T(8,128)(2,1)S(1)}, u32[]{:S(2)}, u32[]{:S(2)}) collective-permute-start(bf16[192,192]{1,0:T(8,128)(2,1)S(1)} %get-tuple-element.34), channel_id=1, source_target_pairs={{2,1},{3,0},{4,7},{5,6},{10,9},{11,8},{12,15},{13,14},{18,17},{19,... | collective-permute-start | bytes 221192 | tf_op jit(solution)/shard_map/ppermute | solution.py:167
  59.4 4.6 %collective-permute-done.15.same = bf16[192,192]{1,0:T(8,128)(2,1)S(1)} collective-permute-done((bf16[192,192]{1,0:T(8,128)(2,1)S(1)}, bf16[192,192]{1,0:T(8,128)(2,1)S(1)}, u32[]{:S(2)}, u32[]{:S(2)}) %collective-permute-start.15) | collective-permute-done | bytes 73760 | tf_op jit(solution)/shard_map/ppermute | solution.py:167
  64.0 1.2 %collective-permute-done.16.cross = bf16[192,192]{1,0:T(8,128)(2,1)S(1)} collective-permute-done((bf16[192,192]{1,0:T(8,128)(2,1)S(1)}, bf16[192,192]{1,0:T(8,128)(2,1)S(1)}, u32[]{:S(2)}, u32[]{:S(2)}) %collective-permute-start.16) | collective-permute-done | bytes 73760 | tf_op jit(solution)/shard_map/ppermute | solution.py:167
  65.1 1.6 %shard_map.35 = f32[192,1024]{1,0:T(8,128)} custom-call(s32[1]{0:T(128)} %bitcast.at_end, f32[192,1024]{1,0:T(8,128)S(1)} %get-tuple-element.30.total, bf16[384,1024]{1,0:T(8,128)(2,1)S(1)} %get-tuple-element.20.s_rows, f32[192,128]{1,0:T(8,128)S(1)} %get-tuple-element.31.norms, bf16[384,1024]{1,0:T(8,128)(2,1)S(1)} %get-tuple-element.32.s_last, ...), custom_call_target="tpu_custom_call" | custom-call | flops 603979776 | bytes 3145728 | tf_op jit(solution)/shard_map/pallas_call | solution.py:155
  (32 shorter events, 4.6 us)
Async XLA Ops:
  0.0 13.2 %collective-permute-start.2 = (bf16[192,1024]{1,0:T(8,128)(2,1)}, bf16[192,1024]{1,0:T(8,128)(2,1)S(1)}, u32[]{:S(2)}, u32[]{:S(2)}) collective-permute-start(bf16[192,1024]{1,0:T(8,128)(2,1)} %s_own.1), channel_id=1, source_target_pairs={{0,2},{1,3},{2,0},{3,1},{4,6},{5,7},{6,4},{7,5},{8,10},{9,11},{10,... | collective-permute-start | bytes 1179656 | tf_op jit(solution)/shard_map/ppermute | solution.py:167
  3.1 17.7 %collective-permute-start.3 = (bf16[192,1024]{1,0:T(8,128)(2,1)}, bf16[192,1024]{1,0:T(8,128)(2,1)S(1)}, u32[]{:S(2)}, u32[]{:S(2)}) collective-permute-start(bf16[192,1024]{1,0:T(8,128)(2,1)} %t_own.1), channel_id=1, source_target_pairs={{0,2},{1,3},{2,0},{3,1},{4,6},{5,7},{6,4},{7,5},{8,10},{9,11},{10,... | collective-permute-start | bytes 1179656 | tf_op jit(solution)/shard_map/ppermute | solution.py:167
  3.1 18.5 %collective-permute-start.4 = (bf16[192,1024]{1,0:T(8,128)(2,1)}, bf16[192,1024]{1,0:T(8,128)(2,1)S(1)}, u32[]{:S(2)}, u32[]{:S(2)}) collective-permute-start(bf16[192,1024]{1,0:T(8,128)(2,1)} %s_own.1), channel_id=1, source_target_pairs={{2,4},{3,5},{4,2},{5,3},{10,12},{11,13},{12,10},{13,11},{18,20},{1... | collective-permute-start | bytes 1179656 | tf_op jit(solution)/shard_map/ppermute | solution.py:167
  3.8 18.3 %collective-permute-start.5 = (bf16[192,1024]{1,0:T(8,128)(2,1)}, bf16[192,1024]{1,0:T(8,128)(2,1)S(1)}, u32[]{:S(2)}, u32[]{:S(2)}) collective-permute-start(bf16[192,1024]{1,0:T(8,128)(2,1)} %t_own.1), channel_id=1, source_target_pairs={{2,4},{3,5},{4,2},{5,3},{10,12},{11,13},{12,10},{13,11},{18,20},{1... | collective-permute-start | bytes 1179656 | tf_op jit(solution)/shard_map/ppermute | solution.py:167
  13.2 9.5 %collective-permute-start.7 = (bf16[192,1024]{1,0:T(8,128)(2,1)S(1)}, bf16[192,1024]{1,0:T(8,128)(2,1)S(1)}, u32[]{:S(2)}, u32[]{:S(2)}) collective-permute-start(bf16[192,1024]{1,0:T(8,128)(2,1)S(1)} %collective-permute-done.2.refs_0_.s_own), channel_id=1, source_target_pairs={{2,3},{3,2},{4,5},{5,4},{10,11},{11,10},{12,13},{13,12},{18,19},{1... | collective-permute-start | bytes 1179656 | tf_op jit(solution)/shard_map/ppermute | solution.py:167
  20.8 3.4 %collective-permute-start.8 = (bf16[192,1024]{1,0:T(8,128)(2,1)S(1)}, bf16[192,1024]{1,0:T(8,128)(2,1)S(1)}, u32[]{:S(2)}, u32[]{:S(2)}) collective-permute-start(bf16[192,1024]{1,0:T(8,128)(2,1)S(1)} %collective-permute-done.3.refs_1_.t_own), channel_id=1, source_target_pairs={{2,3},{3,2},{4,5},{5,4},{10,11},{11,10},{12,13},{13,12},{18,19},{1... | collective-permute-start | bytes 1179656 | tf_op jit(solution)/shard_map/ppermute | solution.py:167
  21.5 7.5 %collective-permute-start = (bf16[192,1024]{1,0:T(8,128)(2,1)}, bf16[192,1024]{1,0:T(8,128)(2,1)S(1)}, u32[]{:S(2)}, u32[]{:S(2)}) collective-permute-start(bf16[192,1024]{1,0:T(8,128)(2,1)} %s_own.1), channel_id=1, source_target_pairs={{0,1},{1,0},{2,3},{3,2},{4,5},{5,4},{6,7},{7,6},{8,9},{9,8},{10,11... | collective-permute-start | bytes 1179656 | tf_op jit(solution)/shard_map/ppermute | solution.py:167
  21.6 8.9 %collective-permute-start.1 = (bf16[192,1024]{1,0:T(8,128)(2,1)}, bf16[192,1024]{1,0:T(8,128)(2,1)S(1)}, u32[]{:S(2)}, u32[]{:S(2)}) collective-permute-start(bf16[192,1024]{1,0:T(8,128)(2,1)} %t_own.1), channel_id=1, source_target_pairs={{0,1},{1,0},{2,3},{3,2},{4,5},{5,4},{6,7},{7,6},{8,9},{9,8},{10,11... | collective-permute-start | bytes 1179656 | tf_op jit(solution)/shard_map/ppermute | solution.py:167
  22.1 12.0 %collective-permute-start.10 = (bf16[192,1024]{1,0:T(8,128)(2,1)S(1)}, bf16[192,1024]{1,0:T(8,128)(2,1)S(1)}, u32[]{:S(2)}, u32[]{:S(2)}) collective-permute-start(bf16[192,1024]{1,0:T(8,128)(2,1)S(1)} %collective-permute-done.2.refs_0_.s_own), channel_id=1, source_target_pairs={{2,4},{3,5},{4,2},{5,3},{10,12},{11,13},{12,10},{13,11},{18,20},{1... | collective-permute-start | bytes 1179656 | tf_op jit(solution)/shard_map/ppermute | solution.py:167
  22.8 0.7 %copy-start.2 = (bf16[192,1024]{1,0:T(8,128)(2,1)}, bf16[192,1024]{1,0:T(8,128)(2,1)S(1)}, u32[]{:S(2)}) copy-start(bf16[192,1024]{1,0:T(8,128)(2,1)S(1)} %collective-permute-done.7.s_other) | copy-start | bytes 1179652
  23.5 11.9 %collective-permute-start.11 = (bf16[192,1024]{1,0:T(8,128)(2,1)S(1)}, bf16[192,1024]{1,0:T(8,128)(2,1)S(1)}, u32[]{:S(2)}, u32[]{:S(2)}) collective-permute-start(bf16[192,1024]{1,0:T(8,128)(2,1)S(1)} %collective-permute-done.3.refs_1_.t_own), channel_id=1, source_target_pairs={{2,4},{3,5},{4,2},{5,3},{10,12},{11,13},{12,10},{13,11},{18,20},{1... | collective-permute-start | bytes 1179656 | tf_op jit(solution)/shard_map/ppermute | solution.py:167
  24.2 0.8 %copy-start.4 = (bf16[192,1024]{1,0:T(8,128)(2,1)}, bf16[192,1024]{1,0:T(8,128)(2,1)S(1)}, u32[]{:S(2)}) copy-start(bf16[192,1024]{1,0:T(8,128)(2,1)S(1)} %collective-permute-done.8.t_other) | copy-start | bytes 1179652
  25.0 19.5 %collective-permute-start.6 = (bf16[192,1024]{1,0:T(8,128)(2,1)S(1)}, bf16[192,1024]{1,0:T(8,128)(2,1)S(1)}, u32[]{:S(2)}, u32[]{:S(2)}) collective-permute-start(bf16[192,1024]{1,0:T(8,128)(2,1)S(1)} %collective-permute-done.4.refs_2_.s_block), channel_id=1, source_target_pairs={{2,0},{3,1},{4,6},{5,7},{10,8},{11,9},{12,14},{13,15},{18,16},{19,... | collective-permute-start | bytes 1179656 | tf_op jit(solution)/shard_map/ppermute | solution.py:167
  26.3 1.0 %copy-start.3 = (bf16[192,1024]{1,0:T(8,128)(2,1)S(1)}, bf16[192,1024]{1,0:T(8,128)(2,1)}, u32[]{:S(2)}) copy-start(bf16[192,1024]{1,0:T(8,128)(2,1)} %copy-done.2) | copy-start | bytes 1179652
  27.3 1.0 %copy-start.5 = (bf16[192,1024]{1,0:T(8,128)(2,1)S(1)}, bf16[192,1024]{1,0:T(8,128)(2,1)}, u32[]{:S(2)}) copy-start(bf16[192,1024]{1,0:T(8,128)(2,1)} %copy-done.4) | copy-start | bytes 1179652
  28.9 1.6 %copy-start = (bf16[192,1024]{1,0:T(8,128)(2,1)S(1)}, bf16[192,1024]{1,0:T(8,128)(2,1)}, u32[]{:S(2)}) copy-start(bf16[192,1024]{1,0:T(8,128)(2,1)} %s_own.1) | copy-start | bytes 1179652
  28.9 1.6 %copy-start.1 = (bf16[192,1024]{1,0:T(8,128)(2,1)S(1)}, bf16[192,1024]{1,0:T(8,128)(2,1)}, u32[]{:S(2)}) copy-start(bf16[192,1024]{1,0:T(8,128)(2,1)} %t_own.1) | copy-start | bytes 1179652
  29.0 17.4 %collective-permute-start.9 = (bf16[192,384]{1,0:T(8,128)(2,1)S(1)}, bf16[192,384]{1,0:T(8,128)(2,1)S(1)}, u32[]{:S(2)}, u32[]{:S(2)}) collective-permute-start(bf16[192,384]{1,0:T(8,128)(2,1)S(1)} %shard_map.31), channel_id=1, source_target_pairs={{2,0},{3,1},{4,6},{5,7},{10,8},{11,9},{12,14},{13,15},{18,16},{19,... | collective-permute-start | bytes 442376 | tf_op jit(solution)/shard_map/ppermute | solution.py:167
  34.1 20.4 %collective-permute-start.13 = (bf16[192,1024]{1,0:T(8,128)(2,1)S(1)}, bf16[192,1024]{1,0:T(8,128)(2,1)S(1)}, u32[]{:S(2)}, u32[]{:S(2)}) collective-permute-start(bf16[192,1024]{1,0:T(8,128)(2,1)S(1)} %collective-permute-done.10.refs_2_.s_block), channel_id=1, source_target_pairs={{2,0},{3,1},{4,6},{5,7},{10,8},{11,9},{12,14},{13,15},{18,16},{19,... | collective-permute-start | bytes 1179656 | tf_op jit(solution)/shard_map/ppermute | solution.py:167
  47.4 11.6 %collective-permute-start.12 = (f32[192,1024]{1,0:T(8,128)S(1)}, f32[192,1024]{1,0:T(8,128)S(1)}, u32[]{:S(2)}, u32[]{:S(2)}) collective-permute-start(f32[192,1024]{1,0:T(8,128)S(1)} %get-tuple-element.29), channel_id=1, source_target_pairs={{0,1},{1,0},{2,3},{3,2},{4,5},{5,4},{6,7},{7,6},{8,9},{9,8},{10,11... | collective-permute-start | bytes 2359304 | tf_op jit(solution)/shard_map/ppermute | solution.py:167
  54.5 4.5 %collective-permute-start.14 = (bf16[192,1024]{1,0:T(8,128)(2,1)S(1)}, bf16[192,1024]{1,0:T(8,128)(2,1)S(1)}, u32[]{:S(2)}, u32[]{:S(2)}) collective-permute-start(bf16[192,1024]{1,0:T(8,128)(2,1)S(1)} %collective-permute-done.13.s_near), channel_id=1, source_target_pairs={{0,1},{1,0},{6,7},{7,6},{8,9},{9,8},{14,15},{15,14},{16,17},{17,16... | collective-permute-start | bytes 1179656 | tf_op jit(solution)/shard_map/ppermute | solution.py:167
  56.4 7.6 %collective-permute-start.15 = (bf16[192,192]{1,0:T(8,128)(2,1)S(1)}, bf16[192,192]{1,0:T(8,128)(2,1)S(1)}, u32[]{:S(2)}, u32[]{:S(2)}) collective-permute-start(bf16[192,192]{1,0:T(8,128)(2,1)S(1)} %get-tuple-element.33), channel_id=1, source_target_pairs={{2,0},{3,1},{4,6},{5,7},{10,8},{11,9},{12,14},{13,15},{18,16},{19,... | collective-permute-start | bytes 221192 | tf_op jit(solution)/shard_map/ppermute | solution.py:167
  57.7 7.4 %collective-permute-start.16 = (bf16[192,192]{1,0:T(8,128)(2,1)S(1)}, bf16[192,192]{1,0:T(8,128)(2,1)S(1)}, u32[]{:S(2)}, u32[]{:S(2)}) collective-permute-start(bf16[192,192]{1,0:T(8,128)(2,1)S(1)} %get-tuple-element.34), channel_id=1, source_target_pairs={{2,1},{3,0},{4,7},{5,6},{10,9},{11,8},{12,15},{13,14},{18,17},{19,... | collective-permute-start | bytes 221192 | tf_op jit(solution)/shard_map/ppermute | solution.py:167
